TPU v7x, 256 devices: a whole 4x4x8 slice. The times are simulated.
256 devices in a mesh: req: 16 (over x, y), seq: 16 (over z, core).
Axes of the slice: x: 4, y: 4, z: 8, core: 2. Of those that a mesh axis runs over, the one named last changes fastest.
Arguments:
- store: bfloat16 [144, 16, 56, 1024], P('req', 'seq'), may hold values from -6 to 6
- passage_owner: int32 [16, 256, 1], P(None, 'seq'), may hold values from 0 to 15; in each aligned block of 16 rows (0 to 15, 16 to 31, ..., all dimensions but the last counted through in order) at most 2 rows name the same one
- passage_slot: int32 [16, 256], P(None, 'seq'), may hold values from 0 to 8
- sel_pos: int32 [16, 1792], P('req'), may hold values from 0 to 14335, as said below
- queries: bfloat16 [16, 1792, 2048], P('req', 'seq'), may hold values from -512 to 512
- new_kv: bfloat16 [16, 1792, 1024], P('req', 'seq'), may hold values from -6 to 6
Outputs:
- blended_kv: bfloat16 [16, 14336, 1024], P('req', 'seq')
- deviation: float32 [16, 1792, 4], P('req', 'seq')
- attended: bfloat16 [16, 1792, 2048], P('req', 'seq')
Inputs may be any that keep to these rules, and one draw needn't show every extreme that they name: `passage_owner`: within the 16 pieces of one request's position block no owner is named more than 2 times, and some block names one owner exactly 2 times. `sel_pos`: entries b * 112 to (b + 1) * 112 - 1 of a request are distinct positions of block b, between b * 896 and (b + 1) * 896 - 1.
All inputs are finite; a program needn't handle non-finite values.
Results may differ from a plain program's by a relative error of at most 0.005.
Values may be sent and summed in bfloat16 or wider, within the bound.
A program may use at most 128 MiB of HBM per device.

v0:
```python
import jax
import jax.numpy as jnp
from jax import lax
from jax.sharding import PartitionSpec as P

HEAD_DIM = 128
KV_HEADS = 4
PASSAGE = 56
PASSAGES_DEV = 16
TOK_DEV = 896
SEL_DEV = 112
Q_WIDTH = 2048
KV_WIDTH = 1024
GROUP = 4


def update(carry_state, query_rows, query_pos, key_rows, value_rows, key_pos):
    running_max, weight_sum, summed = carry_state
    row_count = query_rows.shape[0]
    score_scale = HEAD_DIM ** (-0.5)
    query_split = query_rows.reshape(row_count, KV_HEADS, GROUP, HEAD_DIM)
    scores = (
        jnp.einsum("qkgd,pkd->qkgp", query_split, key_rows, preferred_element_type=jnp.float32)
        * score_scale
    )
    visible = key_pos[None, None, None, :] <= query_pos[:, None, None, None]
    scores = jnp.where(visible, scores, -1e30)
    new_max = jnp.maximum(running_max, jnp.max(scores, axis=-1))
    weights = jnp.where(visible, jnp.exp(scores - new_max[..., None]), 0.0)
    rescale = jnp.exp(running_max - new_max)
    weight_sum = weight_sum * rescale + jnp.sum(weights, axis=-1)
    product = jnp.einsum(
        "qkgp,pkd->qkgd",
        weights.astype(jnp.bfloat16),
        value_rows,
        preferred_element_type=jnp.float32,
    )
    summed = summed * rescale[..., None] + product
    return (new_max, weight_sum, summed)


def fold_attention(groups, blended):
    initial = []
    for query_rows, query_pos in groups:
        row_count = query_rows.shape[0]
        initial.append(
            (
                jnp.full((row_count, KV_HEADS, GROUP), -1e30, jnp.float32),
                jnp.zeros((row_count, KV_HEADS, GROUP), jnp.float32),
                jnp.zeros((row_count, KV_HEADS, GROUP, HEAD_DIM), jnp.float32),
            )
        )
    carry_all = tuple(initial)
    piece = lax.all_gather(blended, "seq", axis=0, tiled=True)
    absorb_row_count = piece.shape[0]
    block_rows = 512

    def take_block(state_all, step_index):
        key_part = lax.dynamic_slice_in_dim(piece, step_index * block_rows, block_rows, 0)
        first_pos = step_index * block_rows
        key_rows = key_part[:, : KV_HEADS * HEAD_DIM].reshape(block_rows, KV_HEADS, HEAD_DIM)
        value_rows = key_part[:, KV_HEADS * HEAD_DIM :].reshape(block_rows, KV_HEADS, HEAD_DIM)
        key_pos = first_pos + jnp.arange(block_rows, dtype=jnp.int32)
        updated = []
        for (query_rows, query_pos), carry_state in zip(groups, state_all):
            updated.append(
                lax.cond(
                    first_pos <= jnp.max(query_pos),
                    lambda state_in: update(
                        state_in, query_rows, query_pos, key_rows, value_rows, key_pos
                    ),
                    lambda state_in: state_in,
                    carry_state,
                )
            )
        return (tuple(updated), None)

    carry_all, _ = lax.scan(take_block, carry_all, jnp.arange(absorb_row_count // block_rows))
    finished = []
    for (query_rows, query_pos), carry_state in zip(groups, carry_all):
        row_count = query_rows.shape[0]
        output_rows = carry_state[2] / carry_state[1][..., None]
        finished.append(output_rows.reshape(row_count, Q_WIDTH).astype(jnp.bfloat16))
    return finished


def body(store, passage_owner, passage_slot, sel_pos, queries, new_kv):
    req_index = lax.axis_index("req")
    seq_index = lax.axis_index("seq")
    owner_table = passage_owner[:, :, 0]
    my_owner = lax.dynamic_index_in_dim(owner_table, req_index, 0, keepdims=False)
    store_shard = store[:, 0]
    req_count = owner_table.shape[0]
    owner_cap = max(2, (2 * PASSAGES_DEV + req_count - 1) // req_count)
    earlier = jnp.arange(PASSAGES_DEV)[:, None] > jnp.arange(PASSAGES_DEV)[None, :]
    same_owner = owner_table[:, :, None] == owner_table[:, None, :]
    rank_table = jnp.sum(same_owner & earlier[None], axis=2)
    slot_hit = (owner_table == req_index)[:, :, None] & (
        rank_table[:, :, None] == jnp.arange(owner_cap)[None, None, :]
    )
    send_slot = jnp.sum(jnp.where(slot_hit, passage_slot[:, :, None], 0), axis=1)
    outgoing = jnp.take(store_shard, send_slot.reshape(-1), axis=0)
    outgoing = outgoing.reshape(req_count, owner_cap, PASSAGE, KV_WIDTH)
    incoming = lax.all_to_all(outgoing, "req", split_axis=0, concat_axis=0, tiled=True)
    my_rank = lax.dynamic_index_in_dim(rank_table, req_index, 0, keepdims=False)
    flat_slot = my_owner * owner_cap + my_rank
    cached = jnp.take(incoming.reshape(req_count * owner_cap, PASSAGE, KV_WIDTH), flat_slot, axis=0)
    cached = cached.reshape(TOK_DEV, KV_WIDTH)
    all_pos = sel_pos[0]
    own_pos = lax.dynamic_slice_in_dim(all_pos, seq_index * SEL_DEV, SEL_DEV)
    offset = own_pos - seq_index * TOK_DEV
    fresh_rows = new_kv[0]
    picked = jnp.take(cached, offset, axis=0)
    blended = cached.at[offset].set(fresh_rows)
    difference = fresh_rows.astype(jnp.float32) - picked.astype(jnp.float32)
    squared = (difference * difference).reshape(SEL_DEV, 2, KV_HEADS, HEAD_DIM)
    deviation = jnp.sum(squared, axis=(1, 3))
    query_local = queries[0]
    attended = fold_attention([(query_local, own_pos)], blended)[0]
    return (blended[None], deviation[None], attended[None])


def solution(mesh):
    placed = (
        P("req", "seq", None, None),
        P(None, "seq", None),
        P(None, "seq"),
        P("req", None),
        P("req", "seq", None),
        P("req", "seq", None),
    )
    return jax.shard_map(
        body,
        mesh=mesh,
        in_specs=placed,
        out_specs=(P("req", "seq", None), P("req", "seq", None), P("req", "seq", None)),
        check_vma=False,
    )
```

profile of v0, /device:TPU:225, one launch (start us, length us, event | category | flops | bytes accessed | tf_op | source)
XLA Modules:
  0.0 505.5 jit_solution(7057776193855823319)
XLA Ops:
  17.2 6.8 %all-to-all-start = ((bf16[16,2,56,1024]{3,2,1,0:T(8,128)(2,1)}), bf16[16,2,56,1024]{3,2,1,0:T(8,128)(2,1)}, u32[]{:S(2)}, u32[]{:S(2)}) async-start(bf16[16,2,56,1024]{3,2,1,0:T(8,128)(2,1)} %broadcast_select_fusion), calls=%async_computation | async-start | bytes 7340032 | tf_op jit(solution)/shard_map/all_to_all | solution.py:104
  27.0 45.7 %all-to-all-done = bf16[16,2,56,1024]{3,2,1,0:T(8,128)(2,1)} async-done(((bf16[16,2,56,1024]{3,2,1,0:T(8,128)(2,1)}), bf16[16,2,56,1024]{3,2,1,0:T(8,128)(2,1)}, u32[]{:S(2)}, u32[]{:S(2)}) %all-to-all-start) | async-done | bytes 3670048 | tf_op jit(solution)/shard_map/all_to_all | solution.py:104
  84.1 158.5 %all-gather.2.cloned.1.call-done = bf16[14336,1024]{1,0:T(8,128)(2,1)} async-done(((bf16[896,1024]{1,0:T(8,128)(2,1)}), bf16[14336,1024]{1,0:T(8,128)(2,1)}) %all-gather.2.cloned.1.call-update) | async-done | bytes 29360144 | tf_op jit(solution)/shard_map/all_gather | solution.py:54
  242.6 35.1 %copy.27 = bf16[14336,1024]{0,1:T(8,128)(2,1)} copy(bf16[14336,1024]{1,0:T(8,128)(2,1)} %all-gather.2.cloned.1.call-done) | data formatting | bytes 58720256 | tf_op jit(solution)/shard_map/while | solution.py:78
  277.8 219.3 %while.15 = (s32[]{:T(128)}, f32[112,4,4]{0,2,1:T(4,128)S(1)}, f32[112,4,4]{0,2,1:T(4,128)S(1)}, f32[112,4,4,128]{3,0,2,1:T(8,128)S(1)}, s32[28]{0:T(128)S(1)}, ...) while((s32[]{:T(128)}, f32[112,4,4]{0,2,1:T(4,128)S(1)}, ...), condition=%wide.region_10.11_spmd, body=%wide.region_5.10_spmd.sunk | while | flops 482209792 | bytes 17720068 | solution.py:78
  279.7 5.9 %conditional.2 = ((f32[112,4,4]{0,2,1:T(4,128)S(1)}, f32[112,4,4]{0,2,1:T(4,128)S(1)}, f32[112,4,4,128]{3,0,2,1:T(8,128)S(1)})) conditional(s32[]{:T(128)} %convert_element_type.61, (f32[112,4,4]{0,2,1:T(4,128)S(1)}, f32[112,4,4]{0,2,1:T(4,128)S(1)}, f32[112,4,4,128]{3,0,2,1:T(8,128)S(1)}) %tuple.51, (s32[]{:T(128)}, s32[512]{0:T(512)S(1)}, ...), branch_computations={%region_6.6_spmd, %region_7.9_spmd} | conditional | flops 482209792 | bytes 17717786 | solution.py:67
  295.4 5.9 %conditional.2 = ((f32[112,4,4]{0,2,1:T(4,128)S(1)}, f32[112,4,4]{0,2,1:T(4,128)S(1)}, f32[112,4,4,128]{3,0,2,1:T(8,128)S(1)})) conditional(s32[]{:T(128)} %convert_element_type.61, (f32[112,4,4]{0,2,1:T(4,128)S(1)}, f32[112,4,4]{0,2,1:T(4,128)S(1)}, f32[112,4,4,128]{3,0,2,1:T(8,128)S(1)}) %tuple.51, (s32[]{:T(128)}, s32[512]{0:T(512)S(1)}, ...), branch_computations={%region_6.6_spmd, %region_7.9_spmd} | conditional | flops 482209792 | bytes 17717786 | solution.py:67
  303.2 5.9 %conditional.2 = ((f32[112,4,4]{0,2,1:T(4,128)S(1)}, f32[112,4,4]{0,2,1:T(4,128)S(1)}, f32[112,4,4,128]{3,0,2,1:T(8,128)S(1)})) conditional(s32[]{:T(128)} %convert_element_type.61, (f32[112,4,4]{0,2,1:T(4,128)S(1)}, f32[112,4,4]{0,2,1:T(4,128)S(1)}, f32[112,4,4,128]{3,0,2,1:T(8,128)S(1)}) %tuple.51, (s32[]{:T(128)}, s32[512]{0:T(512)S(1)}, ...), branch_computations={%region_6.6_spmd, %region_7.9_spmd} | conditional | flops 482209792 | bytes 17717786 | solution.py:67
  311.0 5.9 %conditional.2 = ((f32[112,4,4]{0,2,1:T(4,128)S(1)}, f32[112,4,4]{0,2,1:T(4,128)S(1)}, f32[112,4,4,128]{3,0,2,1:T(8,128)S(1)})) conditional(s32[]{:T(128)} %convert_element_type.61, (f32[112,4,4]{0,2,1:T(4,128)S(1)}, f32[112,4,4]{0,2,1:T(4,128)S(1)}, f32[112,4,4,128]{3,0,2,1:T(8,128)S(1)}) %tuple.51, (s32[]{:T(128)}, s32[512]{0:T(512)S(1)}, ...), branch_computations={%region_6.6_spmd, %region_7.9_spmd} | conditional | flops 482209792 | bytes 17717786 | solution.py:67
  318.9 5.9 %conditional.2 = ((f32[112,4,4]{0,2,1:T(4,128)S(1)}, f32[112,4,4]{0,2,1:T(4,128)S(1)}, f32[112,4,4,128]{3,0,2,1:T(8,128)S(1)})) conditional(s32[]{:T(128)} %convert_element_type.61, (f32[112,4,4]{0,2,1:T(4,128)S(1)}, f32[112,4,4]{0,2,1:T(4,128)S(1)}, f32[112,4,4,128]{3,0,2,1:T(8,128)S(1)}) %tuple.51, (s32[]{:T(128)}, s32[512]{0:T(512)S(1)}, ...), branch_computations={%region_6.6_spmd, %region_7.9_spmd} | conditional | flops 482209792 | bytes 17717786 | solution.py:67
  326.7 5.9 %conditional.2 = ((f32[112,4,4]{0,2,1:T(4,128)S(1)}, f32[112,4,4]{0,2,1:T(4,128)S(1)}, f32[112,4,4,128]{3,0,2,1:T(8,128)S(1)})) conditional(s32[]{:T(128)} %convert_element_type.61, (f32[112,4,4]{0,2,1:T(4,128)S(1)}, f32[112,4,4]{0,2,1:T(4,128)S(1)}, f32[112,4,4,128]{3,0,2,1:T(8,128)S(1)}) %tuple.51, (s32[]{:T(128)}, s32[512]{0:T(512)S(1)}, ...), branch_computations={%region_6.6_spmd, %region_7.9_spmd} | conditional | flops 482209792 | bytes 17717786 | solution.py:67
  334.5 5.9 %conditional.2 = ((f32[112,4,4]{0,2,1:T(4,128)S(1)}, f32[112,4,4]{0,2,1:T(4,128)S(1)}, f32[112,4,4,128]{3,0,2,1:T(8,128)S(1)})) conditional(s32[]{:T(128)} %convert_element_type.61, (f32[112,4,4]{0,2,1:T(4,128)S(1)}, f32[112,4,4]{0,2,1:T(4,128)S(1)}, f32[112,4,4,128]{3,0,2,1:T(8,128)S(1)}) %tuple.51, (s32[]{:T(128)}, s32[512]{0:T(512)S(1)}, ...), branch_computations={%region_6.6_spmd, %region_7.9_spmd} | conditional | flops 482209792 | bytes 17717786 | solution.py:67
  342.4 5.9 %conditional.2 = ((f32[112,4,4]{0,2,1:T(4,128)S(1)}, f32[112,4,4]{0,2,1:T(4,128)S(1)}, f32[112,4,4,128]{3,0,2,1:T(8,128)S(1)})) conditional(s32[]{:T(128)} %convert_element_type.61, (f32[112,4,4]{0,2,1:T(4,128)S(1)}, f32[112,4,4]{0,2,1:T(4,128)S(1)}, f32[112,4,4,128]{3,0,2,1:T(8,128)S(1)}) %tuple.51, (s32[]{:T(128)}, s32[512]{0:T(512)S(1)}, ...), branch_computations={%region_6.6_spmd, %region_7.9_spmd} | conditional | flops 482209792 | bytes 17717786 | solution.py:67
  350.2 5.9 %conditional.2 = ((f32[112,4,4]{0,2,1:T(4,128)S(1)}, f32[112,4,4]{0,2,1:T(4,128)S(1)}, f32[112,4,4,128]{3,0,2,1:T(8,128)S(1)})) conditional(s32[]{:T(128)} %convert_element_type.61, (f32[112,4,4]{0,2,1:T(4,128)S(1)}, f32[112,4,4]{0,2,1:T(4,128)S(1)}, f32[112,4,4,128]{3,0,2,1:T(8,128)S(1)}) %tuple.51, (s32[]{:T(128)}, s32[512]{0:T(512)S(1)}, ...), branch_computations={%region_6.6_spmd, %region_7.9_spmd} | conditional | flops 482209792 | bytes 17717786 | solution.py:67
  358.0 5.9 %conditional.2 = ((f32[112,4,4]{0,2,1:T(4,128)S(1)}, f32[112,4,4]{0,2,1:T(4,128)S(1)}, f32[112,4,4,128]{3,0,2,1:T(8,128)S(1)})) conditional(s32[]{:T(128)} %convert_element_type.61, (f32[112,4,4]{0,2,1:T(4,128)S(1)}, f32[112,4,4]{0,2,1:T(4,128)S(1)}, f32[112,4,4,128]{3,0,2,1:T(8,128)S(1)}) %tuple.51, (s32[]{:T(128)}, s32[512]{0:T(512)S(1)}, ...), branch_computations={%region_6.6_spmd, %region_7.9_spmd} | conditional | flops 482209792 | bytes 17717786 | solution.py:67
  365.9 5.9 %conditional.2 = ((f32[112,4,4]{0,2,1:T(4,128)S(1)}, f32[112,4,4]{0,2,1:T(4,128)S(1)}, f32[112,4,4,128]{3,0,2,1:T(8,128)S(1)})) conditional(s32[]{:T(128)} %convert_element_type.61, (f32[112,4,4]{0,2,1:T(4,128)S(1)}, f32[112,4,4]{0,2,1:T(4,128)S(1)}, f32[112,4,4,128]{3,0,2,1:T(8,128)S(1)}) %tuple.51, (s32[]{:T(128)}, s32[512]{0:T(512)S(1)}, ...), branch_computations={%region_6.6_spmd, %region_7.9_spmd} | conditional | flops 482209792 | bytes 17717786 | solution.py:67
  373.7 5.9 %conditional.2 = ((f32[112,4,4]{0,2,1:T(4,128)S(1)}, f32[112,4,4]{0,2,1:T(4,128)S(1)}, f32[112,4,4,128]{3,0,2,1:T(8,128)S(1)})) conditional(s32[]{:T(128)} %convert_element_type.61, (f32[112,4,4]{0,2,1:T(4,128)S(1)}, f32[112,4,4]{0,2,1:T(4,128)S(1)}, f32[112,4,4,128]{3,0,2,1:T(8,128)S(1)}) %tuple.51, (s32[]{:T(128)}, s32[512]{0:T(512)S(1)}, ...), branch_computations={%region_6.6_spmd, %region_7.9_spmd} | conditional | flops 482209792 | bytes 17717786 | solution.py:67
  381.5 5.9 %conditional.2 = ((f32[112,4,4]{0,2,1:T(4,128)S(1)}, f32[112,4,4]{0,2,1:T(4,128)S(1)}, f32[112,4,4,128]{3,0,2,1:T(8,128)S(1)})) conditional(s32[]{:T(128)} %convert_element_type.61, (f32[112,4,4]{0,2,1:T(4,128)S(1)}, f32[112,4,4]{0,2,1:T(4,128)S(1)}, f32[112,4,4,128]{3,0,2,1:T(8,128)S(1)}) %tuple.51, (s32[]{:T(128)}, s32[512]{0:T(512)S(1)}, ...), branch_computations={%region_6.6_spmd, %region_7.9_spmd} | conditional | flops 482209792 | bytes 17717786 | solution.py:67
  389.4 5.9 %conditional.2 = ((f32[112,4,4]{0,2,1:T(4,128)S(1)}, f32[112,4,4]{0,2,1:T(4,128)S(1)}, f32[112,4,4,128]{3,0,2,1:T(8,128)S(1)})) conditional(s32[]{:T(128)} %convert_element_type.61, (f32[112,4,4]{0,2,1:T(4,128)S(1)}, f32[112,4,4]{0,2,1:T(4,128)S(1)}, f32[112,4,4,128]{3,0,2,1:T(8,128)S(1)}) %tuple.51, (s32[]{:T(128)}, s32[512]{0:T(512)S(1)}, ...), branch_computations={%region_6.6_spmd, %region_7.9_spmd} | conditional | flops 482209792 | bytes 17717786 | solution.py:67
  412.9 5.9 %conditional.2 = ((f32[112,4,4]{0,2,1:T(4,128)S(1)}, f32[112,4,4]{0,2,1:T(4,128)S(1)}, f32[112,4,4,128]{3,0,2,1:T(8,128)S(1)})) conditional(s32[]{:T(128)} %convert_element_type.61, (f32[112,4,4]{0,2,1:T(4,128)S(1)}, f32[112,4,4]{0,2,1:T(4,128)S(1)}, f32[112,4,4,128]{3,0,2,1:T(8,128)S(1)}) %tuple.51, (s32[]{:T(128)}, s32[512]{0:T(512)S(1)}, ...), branch_computations={%region_6.6_spmd, %region_7.9_spmd} | conditional | flops 482209792 | bytes 17717786 | solution.py:67
  436.4 5.9 %conditional.2 = ((f32[112,4,4]{0,2,1:T(4,128)S(1)}, f32[112,4,4]{0,2,1:T(4,128)S(1)}, f32[112,4,4,128]{3,0,2,1:T(8,128)S(1)})) conditional(s32[]{:T(128)} %convert_element_type.61, (f32[112,4,4]{0,2,1:T(4,128)S(1)}, f32[112,4,4]{0,2,1:T(4,128)S(1)}, f32[112,4,4,128]{3,0,2,1:T(8,128)S(1)}) %tuple.51, (s32[]{:T(128)}, s32[512]{0:T(512)S(1)}, ...), branch_computations={%region_6.6_spmd, %region_7.9_spmd} | conditional | flops 482209792 | bytes 17717786 | solution.py:67
  459.9 5.9 %conditional.2 = ((f32[112,4,4]{0,2,1:T(4,128)S(1)}, f32[112,4,4]{0,2,1:T(4,128)S(1)}, f32[112,4,4,128]{3,0,2,1:T(8,128)S(1)})) conditional(s32[]{:T(128)} %convert_element_type.61, (f32[112,4,4]{0,2,1:T(4,128)S(1)}, f32[112,4,4]{0,2,1:T(4,128)S(1)}, f32[112,4,4,128]{3,0,2,1:T(8,128)S(1)}) %tuple.51, (s32[]{:T(128)}, s32[512]{0:T(512)S(1)}, ...), branch_computations={%region_6.6_spmd, %region_7.9_spmd} | conditional | flops 482209792 | bytes 17717786 | solution.py:67
  467.7 5.9 %conditional.2 = ((f32[112,4,4]{0,2,1:T(4,128)S(1)}, f32[112,4,4]{0,2,1:T(4,128)S(1)}, f32[112,4,4,128]{3,0,2,1:T(8,128)S(1)})) conditional(s32[]{:T(128)} %convert_element_type.61, (f32[112,4,4]{0,2,1:T(4,128)S(1)}, f32[112,4,4]{0,2,1:T(4,128)S(1)}, f32[112,4,4,128]{3,0,2,1:T(8,128)S(1)}) %tuple.51, (s32[]{:T(128)}, s32[512]{0:T(512)S(1)}, ...), branch_computations={%region_6.6_spmd, %region_7.9_spmd} | conditional | flops 482209792 | bytes 17717786 | solution.py:67
  483.4 5.9 %conditional.2 = ((f32[112,4,4]{0,2,1:T(4,128)S(1)}, f32[112,4,4]{0,2,1:T(4,128)S(1)}, f32[112,4,4,128]{3,0,2,1:T(8,128)S(1)})) conditional(s32[]{:T(128)} %convert_element_type.61, (f32[112,4,4]{0,2,1:T(4,128)S(1)}, f32[112,4,4]{0,2,1:T(4,128)S(1)}, f32[112,4,4,128]{3,0,2,1:T(8,128)S(1)}) %tuple.51, (s32[]{:T(128)}, s32[512]{0:T(512)S(1)}, ...), branch_computations={%region_6.6_spmd, %region_7.9_spmd} | conditional | flops 482209792 | bytes 17717786 | solution.py:67
  (394 shorter events, 259.7 us)
Async XLA Ops:
  7.2 3.2 copy-start
  17.2 55.5 %all-to-all-start = ((bf16[16,2,56,1024]{3,2,1,0:T(8,128)(2,1)}), bf16[16,2,56,1024]{3,2,1,0:T(8,128)(2,1)}, u32[]{:S(2)}, u32[]{:S(2)}) async-start(bf16[16,2,56,1024]{3,2,1,0:T(8,128)(2,1)} %broadcast_select_fusion), calls=%async_computation | async-start | bytes 7340032 | tf_op jit(solution)/shard_map/all_to_all | solution.py:104
  76.6 2.7 copy-start.4
  79.2 163.4 %all-gather.2.cloned.1.call-start = ((), (), s32[]{:S(2)}) async-start(), calls=%async_computation.1 | async-start | bytes 31195136 | tf_op jit(solution)/shard_map/all_gather | solution.py:54
  81.4 1.2 copy-start.2
  84.1 193.7 %copy-start.3 = (bf16[1,112,2048]{2,1,0:T(8,128)(2,1)S(1)}, bf16[1,112,2048]{2,1,0:T(8,128)(2,1)}, u32[]{:S(2)}) copy-start(bf16[1,112,2048]{2,1,0:T(8,128)(2,1)} %param.14) | copy-start | bytes 1376260
  497.0 1.6 copy-start.1
Sparse Core Ops, SparseCore 0:
  82.8 159.7 all-gather.1
where the time goes:
time: 508 us; the launch traced here: 506 us
  waiting for transfers between devices  204 us (40%)
  local copies, waits for them, and re-layouts  127 us (25%)
  matrix products  65.1 us (13%)
  other arithmetic  49.5 us (10%)
  loops' own time  38.6 us (8%)
  between operations  14.2 us (3%)
  starting transfers between devices  6.84 us (1%)
    all_gather x1, waiting for transfers between devices, fold_attention(): piece = lax.all_gather(blended, 'seq', axis=0, tiled=True)  159 us
    slice x28, local copies, waits for them, and re-layouts, take_block(): key_part[:, KV_HEADS * HEAD_DIM:].reshape(block_rows, KV_HEADS, HEAD_DIM)  52.1 us
    all_to_all x1, waiting for transfers between devices, body(): lax.all_to_all(outgoing, 'req', split_axis=0, concat_axis=0, tiled=True)  45.7 us
    dot_general x28, matrix products, update(): jnp.einsum('qkgp,pkd->qkgd', weights.astype(jnp.bfloat16), value_rows, pr...  42.1 us
    another operation x1, loops' own time, fold_attention(): lax.scan(take_block, carry_all, jnp.arange(absorb_row_count // block_rows))  36.9 us
    while x1, local copies, waits for them, and re-layouts, fold_attention(): lax.scan(take_block, carry_all, jnp.arange(absorb_row_count // block_rows))  35.1 us
    reduce_sum x28, other arithmetic, update(): weight_sum = weight_sum * rescale + jnp.sum(weights, axis=-1)  33.8 us
    dot_general x28, matrix products, update(): jnp.einsum('qkgd,pkd->qkgp', query_split, key_rows, preferred_element_typ...  23.1 us
  transfers between devices with their start and end apart: 2, of which 2 were waited for; matrix products, arithmetic and copies ran while one was open for 1% of the time, Pallas kernels for 0%

commit v1 on v0

--- a/solution.py
+++ b/solution.py
@@ -1,3 +1,4 @@
+import functools
 import jax
 import jax.numpy as jnp
 from jax import lax
@@ -12,6 +13,16 @@
 Q_WIDTH = 2048
 KV_WIDTH = 1024
 GROUP = 4
+
+
+def test_strings_on(x_in, mesh_name):
+    y2 = lax.axis_size(mesh_name)
+    before = jnp.stack([x_in] * y2, axis=0)
+    val2 = lax.all_to_all(before, mesh_name, 0, 0)
+    return jnp.concatenate(val2, 0)
+
+
+rounds_tell = functools.partial(test_strings_on, mesh_name="seq")
 
 
 def update(carry_state, query_rows, query_pos, key_rows, value_rows, key_pos):
@@ -51,7 +62,7 @@
             )
         )
     carry_all = tuple(initial)
-    piece = lax.all_gather(blended, "seq", axis=0, tiled=True)
+    piece = rounds_tell(blended)
     absorb_row_count = piece.shape[0]
     block_rows = 512
 

time: 508 us -> 1030 us (2.03)
  waiting for transfers between devices: 204 us -> 677 us
  local copies, waits for them, and re-layouts: 127 us -> 180 us
  between operations: 14.2 us -> 0.83 us
    all_to_all x0 -> x1, waiting for transfers between devices: none -> 631 us  [test_strings_on(): val2 = lax.all_to_all(before, mesh_name, 0, 0)]
    all_gather x1 -> x0, waiting for transfers between devices: 159 us -> none  [fold_attention(): piece = lax.all_gather(blended, 'seq', axis=0, tiled=True)]
    all_to_all x0 -> x1, local copies, waits for them, and re-layouts: none -> 41 us  [test_strings_on(): val2 = lax.all_to_all(before, mesh_name, 0, 0)]
    another operation x0 -> x1, local copies, waits for them, and re-layouts: none -> 11.1 us  [test_strings_on(): before = jnp.stack([x_in] * y2, axis=0)]
  transfers between devices with their start and end apart: 2 -> 2, of which waited for: 2 -> 2; matrix products, arithmetic and copies ran while one was open for 1% -> 0% of each run, Pallas kernels for 0% -> 0%
where the time goes in v1:
time: 1030 us
  waiting for transfers between devices  677 us (66%)
  local copies, waits for them, and re-layouts  180 us (17%)
  matrix products  65.1 us (6%)
  other arithmetic  49.5 us (5%)
  loops' own time  38.6 us (4%)
  starting transfers between devices  14.1 us (1%)
    all_to_all x1, waiting for transfers between devices, test_strings_on(): val2 = lax.all_to_all(before, mesh_name, 0, 0)  631 us
    slice x28, local copies, waits for them, and re-layouts, take_block(): key_part[:, KV_HEADS * HEAD_DIM:].reshape(block_rows, KV_HEADS, HEAD_DIM)  52.1 us
    all_to_all x1, waiting for transfers between devices, body(): lax.all_to_all(outgoing, 'req', split_axis=0, concat_axis=0, tiled=True)  45.7 us
    dot_general x28, matrix products, update(): jnp.einsum('qkgp,pkd->qkgd', weights.astype(jnp.bfloat16), value_rows, pr...  42.1 us
    all_to_all x1, local copies, waits for them, and re-layouts, test_strings_on(): val2 = lax.all_to_all(before, mesh_name, 0, 0)  41 us
    another operation x1, loops' own time, fold_attention(): lax.scan(take_block, carry_all, jnp.arange(absorb_row_count // block_rows))  36.9 us
    while x1, local copies, waits for them, and re-layouts, fold_attention(): lax.scan(take_block, carry_all, jnp.arange(absorb_row_count // block_rows))  35.1 us
    reduce_sum x28, other arithmetic, update(): weight_sum = weight_sum * rescale + jnp.sum(weights, axis=-1)  33.8 us
  transfers between devices with their start and end apart: 2, of which 2 were waited for; matrix products, arithmetic and copies ran while one was open for 0% of the time, Pallas kernels for 0%

profile of v1, /device:TPU:225, one launch (start us, length us, event | category | flops | bytes accessed | tf_op | source)
XLA Modules:
  0.0 1025.2 jit_solution(7445030610221001740)
XLA Ops:
  10.7 6.8 all-to-all-start
  20.5 45.7 %all-to-all-done = bf16[16,2,56,1024]{3,2,1,0:T(8,128)(2,1)} async-done(((bf16[16,2,56,1024]{3,2,1,0:T(8,128)(2,1)}), bf16[16,2,56,1024]{3,2,1,0:T(8,128)(2,1)}, u32[]{:S(2)}, u32[]{:S(2)}) %all-to-all-start) | async-done | bytes 3670048 | tf_op jit(solution)/shard_map/all_to_all | solution.py:115
  77.4 11.1 %stack.2 = bf16[16,896,1024]{1,2,0:T(8,128)(2,1)} broadcast(bf16[896,1024]{0,1:T(8,128)(2,1)} %copy.35), dimensions={1,2} | broadcast | bytes 31195136 | tf_op jit(solution)/shard_map/stack | solution.py:20
  88.4 7.3 all-to-all-start.1
  97.2 630.9 %all-to-all-done.1 = bf16[16,896,1024]{1,2,0:T(8,128)(2,1)} async-done(((bf16[16,896,1024]{1,2,0:T(8,128)(2,1)}), bf16[16,896,1024]{1,2,0:T(8,128)(2,1)}, u32[]{:S(2)}, u32[]{:S(2)}) %all-to-all-start.1) | async-done | bytes 29360160 | tf_op jit(solution)/shard_map/all_to_all | solution.py:21
  728.1 41.0 %copy.36 = bf16[16,896,1024]{2,1,0:T(8,128)(2,1)} copy(bf16[16,896,1024]{1,2,0:T(8,128)(2,1)} %all-to-all-done.1) | data formatting | bytes 58720256 | tf_op jit(solution)/shard_map/all_to_all | solution.py:21
  769.1 35.1 %copy.37 = bf16[14336,1024]{0,1:T(8,128)(2,1)} copy(bf16[14336,1024]{1,0:T(8,128)(2,1)} %bitcast.78) | data formatting | bytes 58720256 | tf_op jit(solution)/shard_map/while | solution.py:89
  804.3 219.3 %while.15 = (s32[]{:T(128)}, f32[112,4,4]{0,2,1:T(4,128)S(1)}, f32[112,4,4]{0,2,1:T(4,128)S(1)}, f32[112,4,4,128]{3,0,2,1:T(8,128)S(1)}, s32[28]{0:T(128)S(1)}, ...) while((s32[]{:T(128)}, f32[112,4,4]{0,2,1:T(4,128)S(1)}, ...), condition=%wide.region_10.11_spmd, body=%wide.region_5.10_spmd.sunk | while | flops 482209792 | bytes 17720068 | solution.py:89
  806.3 5.9 conditional.2
  814.1 5.9 conditional.2
  821.9 5.9 conditional.2
  829.8 5.9 conditional.2
  837.6 5.9 conditional.2
  845.4 5.9 conditional.2
  853.3 5.9 conditional.2
  861.1 5.9 conditional.2
  876.8 5.9 conditional.2
  900.3 5.9 conditional.2
  915.9 5.9 conditional.2
  923.8 5.9 conditional.2
  947.3 5.9 conditional.2
  970.8 5.9 conditional.2
  994.3 5.9 conditional.2
  1002.1 5.9 conditional.2
  (396 shorter events, 278.6 us)
Async XLA Ops:
  0.6 3.2 copy-start
  10.7 55.5 %all-to-all-start = ((bf16[16,2,56,1024]{3,2,1,0:T(8,128)(2,1)}), bf16[16,2,56,1024]{3,2,1,0:T(8,128)(2,1)}, u32[]{:S(2)}, u32[]{:S(2)}) async-start(bf16[16,2,56,1024]{3,2,1,0:T(8,128)(2,1)} %broadcast_select_fusion), calls=%async_computation | async-start | bytes 7340032 | tf_op jit(solution)/shard_map/all_to_all | solution.py:115
  70.1 2.6 copy-start.4
  74.8 13.6 %copy-start.2 = (bf16[896,1024]{1,0:T(8,128)(2,1)}, bf16[896,1024]{1,0:T(8,128)(2,1)S(1)}, u32[]{:S(2)}) copy-start(bf16[896,1024]{1,0:T(8,128)(2,1)S(1)} %scatter_custom_fusion) | copy-start | bytes 5505028
  88.4 639.6 %all-to-all-start.1 = ((bf16[16,896,1024]{1,2,0:T(8,128)(2,1)}), bf16[16,896,1024]{1,2,0:T(8,128)(2,1)}, u32[]{:S(2)}, u32[]{:S(2)}) async-start(bf16[16,896,1024]{1,2,0:T(8,128)(2,1)} %stack.2), calls=%async_computation.1 | async-start | bytes 58720256 | tf_op jit(solution)/shard_map/all_to_all | solution.py:21
  769.1 35.2 %copy-start.3 = (bf16[1,112,2048]{2,1,0:T(8,128)(2,1)S(1)}, bf16[1,112,2048]{2,1,0:T(8,128)(2,1)}, u32[]{:S(2)}) copy-start(bf16[1,112,2048]{2,1,0:T(8,128)(2,1)} %param.14) | copy-start | bytes 1376260
  1023.6 1.6 copy-start.1
